TPU v7x, 256 devices: a whole 4x4x8 slice. The times are simulated.
256 devices in a mesh: fib: 8 (over y, x_hi), rest: 32 (over z, x_lo, core).
Axes of the slice: x: 4 (x_hi: 2, x_lo: 2; x = x_hi * 2 + x_lo), y: 4, z: 8, core: 2. Of those that a mesh axis runs over, the one named last changes fastest.
Arguments:
- tensor: float32 [64, 128, 64, 1024], P('fib', 'rest'), may hold values from -24 to 24
- factor_one: float32 [1024, 128], replicated, may hold values from 0 to 0.05
- factor_two: float32 [64, 128], P('fib'), may hold values from 0.05 to 0.35
- factor_three: float32 [128, 128], P('rest'), may hold values from 0.03 to 0.25
- factor_four: float32 [64, 128], replicated, may hold values from 0.03 to 0.25
Outputs:
- new_factor: float32 [1024, 128], replicated
- factor_gram: float32 [128, 128], replicated
All inputs are finite; a program needn't handle non-finite values.
Results may differ from a plain program's by a relative error of at most 0.00014.
Values sent between devices are 32-bit elements; how exact they have to be, the bound alone decides.
No kernel may reach another device: no remote copies, remote signals or barrier semaphores. Data moves between devices by JAX's collectives and lax.ppermute only.
A program may use at most 64 MiB of HBM per device.

v0:
```python
import jax
import jax.numpy as jnp
from jax import lax
from jax.sharding import PartitionSpec as P


def from_everyone(value, axis):
    size = lax.axis_size(axis)
    return lax.all_to_all(
        jnp.broadcast_to(value[None], (size, *value.shape)), axis, 0, 0, tiled=True
    )


def of_everyone(value, axis):
    everything = from_everyone(value, axis)
    return jnp.sum(everything, axis=0)


def gathered_total(value, axis):
    return lax.all_gather(value, axis).sum(0)


def hals_columns(factor, mttkrp, gram_v):
    highest = lax.Precision.HIGHEST
    rank_cols = factor.shape[1]
    width = 16
    current = factor
    for block_idx in range(rank_cols // width):
        lower = block_idx * width
        base = jnp.dot(current, gram_v[:, lower : lower + width], precision=highest)
        old_cols = current[:, lower : lower + width]
        inner = gram_v[lower : lower + width, lower : lower + width]
        target = mttkrp[:, lower : lower + width]

        def update(k, cols):
            index = k.astype(jnp.int32)
            zero = jnp.zeros((), jnp.int32)
            inner_col = lax.dynamic_slice_in_dim(inner, index, 1, 1)
            diag = lax.dynamic_slice_in_dim(inner_col, index, 1, 0)[0, 0]
            product = (
                lax.dynamic_slice_in_dim(base, index, 1, 1)[:, 0]
                + jnp.dot(cols - old_cols, inner_col, precision=highest)[:, 0]
            )
            goal = lax.dynamic_slice_in_dim(target, index, 1, 1)[:, 0]
            column = lax.dynamic_slice_in_dim(cols, index, 1, 1)[:, 0]
            fresh = jnp.maximum(column + (goal - product) / diag, 0.0)
            return lax.dynamic_update_slice(cols, fresh[:, None], (zero, index))

        cols = lax.fori_loop(0, width, update, old_cols)
        current = current.at[:, lower : lower + width].set(cols)
    return current


def per_device(tensor, factor_one, factor_two, factor_three, factor_four):
    highest = lax.Precision.HIGHEST
    rank_cols = factor_one.shape[1]
    mode_one = tensor.shape[3]
    khatri = (
        factor_two[:, None, None, :]
        * factor_three[None, :, None, :]
        * factor_four[None, None, :, :]
    ).reshape(-1, rank_cols)
    flat = tensor.reshape(-1, mode_one)
    part_two = jnp.dot(factor_two.T, factor_two, precision=highest)
    part_three = jnp.dot(factor_three.T, factor_three, precision=highest)
    gram_four = jnp.dot(factor_four.T, factor_four, precision=highest)
    gram_two = of_everyone(part_two, "fib")
    gram_three = gathered_total(part_three, "rest")
    gram_v = gram_two * gram_three * gram_four
    partial_value = lax.dot_general(flat, khatri, (((0,), (0,)), ((), ())), precision=highest)
    mttkrp = lax.psum(partial_value, ("fib", "rest"))
    new_factor = hals_columns(factor_one, mttkrp, gram_v)
    factor_gram = jnp.dot(new_factor.T, new_factor, precision=highest)
    return (new_factor, factor_gram)


def solution(mesh):
    return jax.shard_map(
        per_device,
        mesh=mesh,
        in_specs=(P("fib", "rest", None, None), P(), P("fib", None), P("rest", None), P()),
        out_specs=(P(), P()),
        check_vma=False,
    )
```

profile of v0, /device:TPU:2, one launch (start us, length us, event | category | flops | bytes accessed | tf_op | source)
XLA Modules:
  0.0 526.8 jit_solution(3609673047529688155)
XLA Ops:
  8.1 1.0 copy.149
  9.8 7.8 %convolution_bitcast_fusion.8 = f32[1024,128]{0,1:T(8,128)} fusion(f32[8,4,64,1024]{3,2,1,0:T(8,128)} %param.37, f32[64,128]{1,0:T(8,128)} %param.41, f32[8,4,128]{2,1,0:T(4,128)S(1)} %broadcast_multiply_fusion), kind=kOutput, calls=%fused_computation.64 | convolution fusion | flops 3221487616 | bytes 8962048 | tf_op jit(solution)/shard_map/dot_general | solution.py:70
  17.8 0.9 fusion.69
  19.0 0.8 broadcast_in_dim.33
  19.9 6.0 %all-to-all-start = ((f32[8,128,128]{2,1,0:T(8,128)}), f32[8,128,128]{2,1,0:T(8,128)S(1)}, u32[]{:S(2)}, u32[]{:S(2)}) async-start(f32[8,128,128]{2,1,0:T(8,128)} %broadcast_in_dim.33), calls=%async_computation | async-start | bytes 1048576 | tf_op jit(solution)/shard_map/all_to_all | solution.py:9
  30.8 246.9 %all-reduce.2.cloned.1.call-done = f32[1024,128]{0,1:T(8,128)} async-done(((f32[1024,128]{0,1:T(8,128)}), f32[1024,128]{0,1:T(8,128)}) %all-reduce.2.cloned.1.call-update) | async-done | bytes 524304 | tf_op jit(solution)/shard_map/psum | solution.py:71
  277.7 1.1 fusion.66
  279.0 1.7 reduce_sum.19
  281.7 24.8 %while.136 = (s32[]{:T(128)}, f32[1024,16]{0,1:T(8,128)S(1)}, f32[1024,16]{0,1:T(8,128)S(1)}, f32[1024,16]{0,1:T(8,128)S(1)}, f32[1024,16]{0,1:T(8,128)S(1)}, /*...) while((s32[]{:T(128)}, f32[1024,16]{0,1:T(8,128)S(1)}, f32[1024,16]{0,1:T(8,128)S(1)}, ...), condition=%wide.region_5.0_spmd, body=%wide.region_4.0_spmd.sunk | while | flops 218115 | bytes 157821 | solution.py:49
  285.4 0.8 fusion.105
  290.0 0.8 fusion.105
  294.7 0.8 fusion.105
  307.4 2.3 scatter.26
  310.6 24.8 %while.137 = (s32[]{:T(128)}, f32[1024,16]{0,1:T(8,128)S(1)}, f32[1024,16]{0,1:T(8,128)S(1)}, f32[1024,16]{0,1:T(8,128)S(1)}, f32[1024,16]{0,1:T(8,128)S(1)}, /*...) while((s32[]{:T(128)}, f32[1024,16]{0,1:T(8,128)S(1)}, f32[1024,16]{0,1:T(8,128)S(1)}, ...), condition=%wide.region_8.0_spmd, body=%wide.region_7.0_spmd.sunk | while | flops 218115 | bytes 157821 | solution.py:49
  335.6 0.8 broadcast_select_fusion.5
  336.4 3.1 scatter.29
  340.4 24.8 %while.138 = (s32[]{:T(128)}, f32[1024,16]{0,1:T(8,128)S(1)}, f32[1024,16]{0,1:T(8,128)S(1)}, f32[1024,16]{0,1:T(8,128)S(1)}, f32[1024,16]{0,1:T(8,128)S(1)}, /*...) while((s32[]{:T(128)}, f32[1024,16]{0,1:T(8,128)S(1)}, f32[1024,16]{0,1:T(8,128)S(1)}, ...), condition=%wide.region_11.0_spmd, body=%wide.region_10.0_spmd.sunk | while | flops 218115 | bytes 157821 | solution.py:49
  365.4 0.8 broadcast_select_fusion.4
  366.3 3.1 scatter.30
  370.3 24.7 %while.139 = (s32[]{:T(128)}, f32[1024,16]{0,1:T(8,128)S(1)}, f32[1024,16]{0,1:T(8,128)S(1)}, f32[1024,16]{0,1:T(8,128)S(1)}, f32[1024,16]{0,1:T(8,128)S(1)}, /*...) while((s32[]{:T(128)}, f32[1024,16]{0,1:T(8,128)S(1)}, f32[1024,16]{0,1:T(8,128)S(1)}, ...), condition=%wide.region_14.0_spmd, body=%wide.region_13.0_spmd.sunk | while | flops 218115 | bytes 157821 | solution.py:49
  396.0 3.1 scatter.31
  400.0 24.8 %while.140 = (s32[]{:T(128)}, f32[1024,16]{0,1:T(8,128)S(1)}, f32[1024,16]{0,1:T(8,128)S(1)}, f32[1024,16]{0,1:T(8,128)S(1)}, f32[1024,16]{0,1:T(8,128)S(1)}, /*...) while((s32[]{:T(128)}, f32[1024,16]{0,1:T(8,128)S(1)}, f32[1024,16]{0,1:T(8,128)S(1)}, ...), condition=%wide.region_17.0_spmd, body=%wide.region_16.0_spmd.sunk | while | flops 218115 | bytes 157821 | solution.py:49
  425.0 0.9 broadcast_select_fusion.2
  425.8 3.1 scatter.34
  429.8 24.7 %while.141 = (s32[]{:T(128)}, f32[1024,16]{0,1:T(8,128)S(1)}, f32[1024,16]{0,1:T(8,128)S(1)}, f32[1024,16]{0,1:T(8,128)S(1)}, f32[1024,16]{0,1:T(8,128)S(1)}, /*...) while((s32[]{:T(128)}, f32[1024,16]{0,1:T(8,128)S(1)}, f32[1024,16]{0,1:T(8,128)S(1)}, ...), condition=%wide.region_20.0_spmd, body=%wide.region_19.0_spmd.sunk | while | flops 218115 | bytes 157821 | solution.py:49
  455.6 3.1 scatter.35
  459.6 24.7 %while.142 = (s32[]{:T(128)}, f32[1024,16]{0,1:T(8,128)S(1)}, f32[1024,16]{0,1:T(8,128)S(1)}, f32[1024,16]{0,1:T(8,128)S(1)}, f32[1024,16]{0,1:T(8,128)S(1)}, /*...) while((s32[]{:T(128)}, f32[1024,16]{0,1:T(8,128)S(1)}, f32[1024,16]{0,1:T(8,128)S(1)}, ...), condition=%wide.region_23.0_spmd, body=%wide.region_22.0_spmd.sunk | while | flops 218115 | bytes 157821 | solution.py:49
  484.5 0.9 broadcast_select_fusion
  485.4 3.3 scatter.36
  489.6 24.8 %while.143 = (s32[]{:T(128)}, f32[1024,16]{0,1:T(8,128)S(1)}, f32[1024,16]{0,1:T(8,128)S(1)}, f32[1024,16]{0,1:T(8,128)S(1)}, f32[1024,16]{0,1:T(8,128)S(1)}, /*...) while((s32[]{:T(128)}, f32[1024,16]{0,1:T(8,128)S(1)}, f32[1024,16]{0,1:T(8,128)S(1)}, ...), condition=%wide.region_25.0_spmd, body=%wide.region_24.0_spmd.sunk | while | flops 218115 | bytes 157821 | solution.py:49
  514.6 3.1 scatter.39
  517.7 1.6 fusion.70
  (451 shorter events, 208.9 us)
Async XLA Ops:
  8.0 10.7 %copy-start.2 = (f32[8,128]{1,0:T(8,128)S(1)}, f32[8,128]{1,0:T(8,128)}, u32[]{:S(2)}) copy-start(f32[8,128]{1,0:T(8,128)} %param.39) | copy-start | bytes 12292
  8.0 9.7 %copy-start.3 = (f32[4,128]{1,0:T(4,128)S(1)}, f32[4,128]{1,0:T(4,128)}, u32[]{:S(2)}) copy-start(f32[4,128]{1,0:T(4,128)} %param.40) | copy-start | bytes 6148
  8.0 272.8 %copy-start.1 = (f32[64,128]{1,0:T(8,128)S(1)}, f32[64,128]{1,0:T(8,128)}, u32[]{:S(2)}) copy-start(f32[64,128]{1,0:T(8,128)} %param.41) | copy-start | bytes 98308
  8.0 269.7 %all-reduce.2.cloned.1.call-start = ((), (), s32[]{:S(2)}) async-start(), calls=%async_computation.1 | async-start | bytes 1048576 | tf_op jit(solution)/shard_map/psum | solution.py:71
  17.7 261.3 %all-gather.3.cloned.1.call-start = ((), (), s32[]{:S(2)}) async-start(), calls=%async_computation.2 | async-start | bytes 2162688 | tf_op jit(solution)/shard_map/all_gather | solution.py:20
  19.9 258.9 %all-to-all-start = ((f32[8,128,128]{2,1,0:T(8,128)}), f32[8,128,128]{2,1,0:T(8,128)S(1)}, u32[]{:S(2)}, u32[]{:S(2)}) async-start(f32[8,128,128]{2,1,0:T(8,128)} %broadcast_in_dim.33), calls=%async_computation | async-start | bytes 1048576 | tf_op jit(solution)/shard_map/all_to_all | solution.py:9
  517.7 1.7 copy-start
Sparse Core Ops, SparseCore 0:
  17.8 259.8 all-reduce.1
Sparse Core Ops, SparseCore 1:
  20.6 66.9 all-gather.2
where the time goes:
time: 528 us; the launch traced here: 527 us
  waiting for transfers between devices  247 us (47%)
  local copies, waits for them, and re-layouts  121 us (23%)
  matrix products  120 us (23%)
  between operations  15.8 us (3%)
  other arithmetic  12.8 us (2%)
  starting transfers between devices  6.11 us (1%)
    psum x1, waiting for transfers between devices, per_device(): mttkrp = lax.psum(partial_value, ('fib', 'rest'))  247 us
    dot_general x128, matrix products, update(): jnp.dot(cols - old_cols, inner_col, precision=highest)[:, 0]  104 us
    dynamic_slice x128, local copies, waits for them, and re-layouts, update(): diag = lax.dynamic_slice_in_dim(inner_col, index, 1, 0)[0, 0]  75.3 us
    scatter x8, local copies, waits for them, and re-layouts, hals_columns(): current = current.at[:, lower:lower + width].set(cols)  23.9 us
    dynamic_update_slice x128, local copies, waits for them, and re-layouts, update(): return lax.dynamic_update_slice(cols, fresh[:, None], (zero, index))  14.1 us
  transfers between devices with their start and end apart: 3, of which 1 were waited for; matrix products, arithmetic and copies ran while one was open for 2% of the time, Pallas kernels for 0%

commit v1 on v0

--- a/solution.py
+++ b/solution.py
@@ -68,7 +68,8 @@
     gram_three = gathered_total(part_three, "rest")
     gram_v = gram_two * gram_three * gram_four
     partial_value = lax.dot_general(flat, khatri, (((0,), (0,)), ((), ())), precision=highest)
-    mttkrp = lax.psum(partial_value, ("fib", "rest"))
+    half = lax.psum(partial_value, "fib")
+    mttkrp = lax.psum(half, "rest")
     new_factor = hals_columns(factor_one, mttkrp, gram_v)
     factor_gram = jnp.dot(new_factor.T, new_factor, precision=highest)
     return (new_factor, factor_gram)

time: 528 us -> 657 us (1.24)
  waiting for transfers between devices: 247 us -> 377 us
    all_gather x1, waiting for transfers between devices: 0.03 us -> 69.1 us  [gathered_total(): return lax.all_gather(value, axis).sum(0)]
    psum x1 -> x2, waiting for transfers between devices: 247 us -> 303 us  [the longest x1 209 us: per_device(): mttkrp = lax.psum(half, 'rest')]
  transfers between devices with their start and end apart: 3 -> 4, of which waited for: 1 -> 4; matrix products, arithmetic and copies ran while one was open for 2% -> 1% of each run, Pallas kernels for 0% -> 0%
where the time goes in v1:
time: 657 us; the launch traced here: 653 us
  waiting for transfers between devices  377 us (57%)
  local copies, waits for them, and re-layouts  121 us (18%)
  matrix products  120 us (18%)
  between operations  14.1 us (2%)
  other arithmetic  12.8 us (2%)
    psum x1, waiting for transfers between devices, per_device(): mttkrp = lax.psum(half, 'rest')  209 us
    dot_general x128, matrix products, update(): jnp.dot(cols - old_cols, inner_col, precision=highest)[:, 0]  104 us
    psum x1, waiting for transfers between devices, per_device(): half = lax.psum(partial_value, 'fib')  93.7 us
    dynamic_slice x128, local copies, waits for them, and re-layouts, update(): diag = lax.dynamic_slice_in_dim(inner_col, index, 1, 0)[0, 0]  75.3 us
    all_gather x1, waiting for transfers between devices, gathered_total(): return lax.all_gather(value, axis).sum(0)  69.1 us
    scatter x8, local copies, waits for them, and re-layouts, hals_columns(): current = current.at[:, lower:lower + width].set(cols)  23.9 us
    dynamic_update_slice x128, local copies, waits for them, and re-layouts, update(): return lax.dynamic_update_slice(cols, fresh[:, None], (zero, index))  14.1 us
  transfers between devices with their start and end apart: 4, of which 4 were waited for; matrix products, arithmetic and copies ran while one was open for 1% of the time, Pallas kernels for 0%

profile of v1, /device:TPU:2, one launch (start us, length us, event | category | flops | bytes accessed | tf_op | source)
XLA Modules:
  0.0 653.2 jit_solution(8107987271859167956)
XLA Ops:
  7.2 1.0 copy.150
  9.0 7.8 %convolution_bitcast_fusion.8 = f32[1024,128]{0,1:T(8,128)} fusion(f32[8,4,64,1024]{3,2,1,0:T(8,128)} %param.37, f32[64,128]{1,0:T(8,128)} %param.41, f32[8,4,128]{2,1,0:T(4,128)S(1)} %broadcast_multiply_fusion), kind=kOutput, calls=%fused_computation.64 | convolution fusion | flops 3221487616 | bytes 8962048 | tf_op jit(solution)/shard_map/dot_general | solution.py:70
  16.9 93.7 %all-reduce.3.cloned.1.call-done = f32[1024,128]{0,1:T(8,128)} async-done(((f32[1024,128]{0,1:T(8,128)}), f32[1024,128]{0,1:T(8,128)}) %all-reduce.3.cloned.1.call-update) | async-done | bytes 524304 | tf_op jit(solution)/shard_map/psum | solution.py:71
  110.7 0.9 fusion.69
  112.0 0.8 broadcast_in_dim.33
  112.8 3.7 all-to-all-start
  121.4 5.1 all-to-all-done
  126.6 209.4 %all-reduce.5.cloned.1.call-done = f32[1024,128]{0,1:T(8,128)} async-done(((f32[1024,128]{0,1:T(8,128)}), f32[1024,128]{0,1:T(8,128)}) %all-reduce.5.cloned.1.call-update) | async-done | bytes 524304 | tf_op jit(solution)/shard_map/psum | solution.py:72
  336.0 1.1 fusion.66
  337.1 69.1 %all-gather.3.cloned.1.call-done = f32[4096,128]{1,0:T(8,128)} async-done(((f32[128,128]{1,0:T(8,128)}), f32[4096,128]{1,0:T(8,128)}) %all-gather.3.cloned.1.call-update) | async-done | bytes 2097168 | tf_op jit(solution)/shard_map/all_gather | solution.py:20
  406.3 1.7 reduce_sum.19
  409.0 24.8 %while.136 = (s32[]{:T(128)}, f32[1024,16]{0,1:T(8,128)S(1)}, f32[1024,16]{0,1:T(8,128)S(1)}, f32[1024,16]{0,1:T(8,128)S(1)}, f32[1024,16]{0,1:T(8,128)S(1)}, /*...) while((s32[]{:T(128)}, f32[1024,16]{0,1:T(8,128)S(1)}, f32[1024,16]{0,1:T(8,128)S(1)}, ...), condition=%wide.region_6.0_spmd, body=%wide.region_5.0_spmd.sunk | while | flops 218115 | bytes 157821 | solution.py:49
  434.7 2.3 scatter.26
  437.9 24.8 %while.137 = (s32[]{:T(128)}, f32[1024,16]{0,1:T(8,128)S(1)}, f32[1024,16]{0,1:T(8,128)S(1)}, f32[1024,16]{0,1:T(8,128)S(1)}, f32[1024,16]{0,1:T(8,128)S(1)}, /*...) while((s32[]{:T(128)}, f32[1024,16]{0,1:T(8,128)S(1)}, f32[1024,16]{0,1:T(8,128)S(1)}, ...), condition=%wide.region_9.0_spmd, body=%wide.region_8.0_spmd.sunk | while | flops 218115 | bytes 157821 | solution.py:49
  462.9 0.8 broadcast_select_fusion.5
  463.7 3.1 scatter.29
  467.7 24.8 %while.138 = (s32[]{:T(128)}, f32[1024,16]{0,1:T(8,128)S(1)}, f32[1024,16]{0,1:T(8,128)S(1)}, f32[1024,16]{0,1:T(8,128)S(1)}, f32[1024,16]{0,1:T(8,128)S(1)}, /*...) while((s32[]{:T(128)}, f32[1024,16]{0,1:T(8,128)S(1)}, f32[1024,16]{0,1:T(8,128)S(1)}, ...), condition=%wide.region_12.0_spmd, body=%wide.region_11.0_spmd.sunk | while | flops 218115 | bytes 157821 | solution.py:49
  492.7 0.8 broadcast_select_fusion.4
  493.5 3.1 scatter.30
  497.5 24.7 %while.139 = (s32[]{:T(128)}, f32[1024,16]{0,1:T(8,128)S(1)}, f32[1024,16]{0,1:T(8,128)S(1)}, f32[1024,16]{0,1:T(8,128)S(1)}, f32[1024,16]{0,1:T(8,128)S(1)}, /*...) while((s32[]{:T(128)}, f32[1024,16]{0,1:T(8,128)S(1)}, f32[1024,16]{0,1:T(8,128)S(1)}, ...), condition=%wide.region_15.0_spmd, body=%wide.region_14.0_spmd.sunk | while | flops 218115 | bytes 157821 | solution.py:49
  523.3 3.1 scatter.31
  527.3 24.8 %while.140 = (s32[]{:T(128)}, f32[1024,16]{0,1:T(8,128)S(1)}, f32[1024,16]{0,1:T(8,128)S(1)}, f32[1024,16]{0,1:T(8,128)S(1)}, f32[1024,16]{0,1:T(8,128)S(1)}, /*...) while((s32[]{:T(128)}, f32[1024,16]{0,1:T(8,128)S(1)}, f32[1024,16]{0,1:T(8,128)S(1)}, ...), condition=%wide.region_18.0_spmd, body=%wide.region_17.0_spmd.sunk | while | flops 218115 | bytes 157821 | solution.py:49
  552.2 0.9 broadcast_select_fusion.2
  553.1 3.1 scatter.34
  557.1 24.7 %while.141 = (s32[]{:T(128)}, f32[1024,16]{0,1:T(8,128)S(1)}, f32[1024,16]{0,1:T(8,128)S(1)}, f32[1024,16]{0,1:T(8,128)S(1)}, f32[1024,16]{0,1:T(8,128)S(1)}, /*...) while((s32[]{:T(128)}, f32[1024,16]{0,1:T(8,128)S(1)}, f32[1024,16]{0,1:T(8,128)S(1)}, ...), condition=%wide.region_21.0_spmd, body=%wide.region_20.0_spmd.sunk | while | flops 218115 | bytes 157821 | solution.py:49
  582.8 3.1 scatter.35
  586.8 24.7 %while.142 = (s32[]{:T(128)}, f32[1024,16]{0,1:T(8,128)S(1)}, f32[1024,16]{0,1:T(8,128)S(1)}, f32[1024,16]{0,1:T(8,128)S(1)}, f32[1024,16]{0,1:T(8,128)S(1)}, /*...) while((s32[]{:T(128)}, f32[1024,16]{0,1:T(8,128)S(1)}, f32[1024,16]{0,1:T(8,128)S(1)}, ...), condition=%wide.region_24.0_spmd, body=%wide.region_23.0_spmd.sunk | while | flops 218115 | bytes 157821 | solution.py:49
  611.8 0.9 broadcast_select_fusion
  612.7 3.3 scatter.36
  616.9 24.8 %while.143 = (s32[]{:T(128)}, f32[1024,16]{0,1:T(8,128)S(1)}, f32[1024,16]{0,1:T(8,128)S(1)}, f32[1024,16]{0,1:T(8,128)S(1)}, f32[1024,16]{0,1:T(8,128)S(1)}, /*...) while((s32[]{:T(128)}, f32[1024,16]{0,1:T(8,128)S(1)}, f32[1024,16]{0,1:T(8,128)S(1)}, ...), condition=%wide.region_26.0_spmd, body=%wide.region_25.0_spmd.sunk | while | flops 218115 | bytes 157821 | solution.py:49
  641.9 3.1 scatter.39
  645.0 1.6 fusion.70
  (454 shorter events, 211.4 us)
Async XLA Ops:
  7.2 104.5 %copy-start.2 = (f32[8,128]{1,0:T(8,128)S(1)}, f32[8,128]{1,0:T(8,128)}, u32[]{:S(2)}) copy-start(f32[8,128]{1,0:T(8,128)} %param.39) | copy-start | bytes 12292
  7.2 103.5 %copy-start.3 = (f32[4,128]{1,0:T(4,128)S(1)}, f32[4,128]{1,0:T(4,128)}, u32[]{:S(2)}) copy-start(f32[4,128]{1,0:T(4,128)} %param.40) | copy-start | bytes 6148
  7.2 103.5 %all-reduce.3.cloned.1.call-start = ((), (), s32[]{:S(2)}) async-start(), calls=%async_computation.1 | async-start | bytes 1048576 | tf_op jit(solution)/shard_map/psum | solution.py:71
  8.3 399.8 %copy-start.1 = (f32[64,128]{1,0:T(8,128)S(1)}, f32[64,128]{1,0:T(8,128)}, u32[]{:S(2)}) copy-start(f32[64,128]{1,0:T(8,128)} %param.41) | copy-start | bytes 98308
  16.9 319.2 %all-reduce.5.cloned.1.call-start = ((), (), s32[]{:S(2)}) async-start(), calls=%async_computation.2 | async-start | bytes 1048576 | tf_op jit(solution)/shard_map/psum | solution.py:72
  110.7 295.6 %all-gather.3.cloned.1.call-start = ((), (), s32[]{:S(2)}) async-start(), calls=%async_computation.3 | async-start | bytes 2162688 | tf_op jit(solution)/shard_map/all_gather | solution.py:20
  112.8 13.7 %all-to-all-start = ((f32[8,128,128]{2,1,0:T(8,128)}), f32[8,128,128]{2,1,0:T(8,128)S(1)}, u32[]{:S(2)}, u32[]{:S(2)}) async-start(f32[8,128,128]{2,1,0:T(8,128)} %broadcast_in_dim.33), calls=%async_computation | async-start | bytes 1048576 | tf_op jit(solution)/shard_map/all_to_all | solution.py:9
  645.0 1.7 copy-start
Sparse Core Ops, SparseCore 0:
  17.0 93.6 all-reduce.2
  113.3 222.7 all-reduce.4
  338.5 67.7 all-gather.2
